TPU v7x, 512 devices: a whole 4x4x16 slice. The times are simulated.
512 devices in a mesh: ctx: 16 (over x, y), ep: 32 (over z, core).
Axes of the slice: x: 4, y: 4, z: 16, core: 2. Of those that a mesh axis runs over, the one named last changes fastest.
Arguments:
- queries: bfloat16 [32, 2048, 4096], P('ep', 'ctx'), may hold values from -7 to 7
- keys: bfloat16 [32, 2048, 256], P('ep', 'ctx'), may hold values from -4.5 to 4.5
- values: bfloat16 [32, 2048, 256], P('ep', 'ctx'), may hold values from -5 to 5
- hidden: bfloat16 [32, 2048, 2048], P('ep', 'ctx'), may hold values from -130 to 130
- expert_ids: int32 [32, 2048, 2], P('ep', 'ctx'), may hold values from 0 to 31, all different within a row; in each aligned block of 128 rows (0 to 127, 128 to 255, ..., all dimensions but the last counted through in order) at most 12 rows name the same one
- gate_probs: float32 [32, 2048, 2], P('ep', 'ctx'), may hold values from 0.2 to 1
- norm_gain: float32 [2048], replicated, may hold values from 0.1 to 1.9
- w_gate: bfloat16 [32, 768, 2048], P('ep', 'ctx'), may hold values from -0.125 to 0.125
- w_up: bfloat16 [32, 768, 2048], P('ep', 'ctx'), may hold values from -0.125 to 0.125
- w_down: bfloat16 [32, 768, 2048], P('ep', 'ctx'), may hold values from -0.21875 to 0.21875
Outputs:
- attended: bfloat16 [32, 2048, 4096], P('ep', 'ctx')
- expert_mix: bfloat16 [32, 2048, 2048], P('ep', 'ctx')
Inputs may be any that keep to these rules, and one draw needn't show every extreme that they name: `expert_ids`: the 2 experts of one token differ. Among the 128 tokens of one device no expert is named more than 12 times.
All inputs are finite; a program needn't handle non-finite values.
Results may differ from a plain program's by a relative error of at most 0.0071.
Values may be sent and summed in bfloat16 or wider, within the bound.
No kernel may reach another device: no remote copies, remote signals or barrier semaphores. Data moves between devices by JAX's collectives and lax.ppermute only.
A program may use at most 128 MiB of HBM per device.

v0:
```python
import math
import jax
import jax.numpy as jnp
from jax import lax
from jax.sharding import PartitionSpec as P

HQ = 32
KVH = 2
DH = 128


def attend(queries, keys, values):
    row_count = queries.shape[1]
    head_ratio = HQ // KVH
    score_factor = 1.0 / math.sqrt(DH)
    my_index = lax.axis_index("ctx")
    query_heads = queries[0].reshape(row_count, KVH, head_ratio, DH)
    groups = [(query_heads, my_index * row_count + jnp.arange(row_count, dtype=jnp.int32))]
    initial = tuple(
        (
            (
                jnp.full((KVH, head_ratio, group_rows.shape[0]), -1e30, jnp.float32),
                jnp.zeros((KVH, head_ratio, group_rows.shape[0]), jnp.float32),
                jnp.zeros((KVH, head_ratio, group_rows.shape[0], DH), jnp.float32),
            )
            for group_rows, group_pos in groups
        )
    )

    def update(carried, pieces_in, offset):
        key_piece, value_piece = pieces_in
        piece_rows = key_piece.shape[0]
        key_heads = key_piece.reshape(piece_rows, KVH, DH)
        value_heads = value_piece.reshape(piece_rows, KVH, DH)
        key_pos = jnp.arange(piece_rows, dtype=jnp.int32)
        updated = []
        for (group_rows, query_pos), current in zip(groups, carried):

            def compute(present, group_rows=group_rows, query_pos=query_pos):
                maxima, totals, weighted = present
                scores = (
                    jnp.einsum(
                        "rgjd,ngd->gjrn", group_rows, key_heads, preferred_element_type=jnp.float32
                    )
                    * score_factor
                )
                visible = key_pos[None, :] <= query_pos[:, None]
                scores = jnp.where(visible, scores, -jnp.inf)
                new_maxima = jnp.maximum(maxima, jnp.max(scores, axis=-1))
                exponent = jnp.exp(scores - new_maxima[..., None])
                new_totals = jnp.sum(exponent, axis=-1)
                product = jnp.einsum(
                    "gjrn,ngd->gjrd",
                    exponent.astype(jnp.bfloat16),
                    value_heads,
                    preferred_element_type=jnp.float32,
                )
                return (new_maxima, new_totals, product)

            def unchanged(present):
                return present

            updated.append(lax.cond(offset <= jnp.max(query_pos), compute, unchanged, current))
        return tuple(updated)

    finals = update(
        initial,
        (
            lax.all_gather(keys[0], "ctx", axis=0, tiled=True),
            lax.all_gather(values[0], "ctx", axis=0, tiled=True),
        ),
        jnp.int32(0),
    )
    outputs = []
    for (group_rows, query_pos), final_state in zip(groups, finals):
        maxima, totals, weighted = final_state
        result = weighted / totals[..., None]
        result = jnp.transpose(result, (2, 0, 1, 3)).reshape(group_rows.shape[0], HQ * DH)
        outputs.append(result.astype(jnp.bfloat16))
    merged = outputs[0]
    return merged[None]


def experts(hidden, expert_ids, gate_probs, norm_gain, w_gate, w_up, w_down):
    tokens = hidden[0].astype(jnp.float32)
    row_count = tokens.shape[0]
    route_count = expert_ids.shape[2]
    expert_count = lax.axis_size("ep")
    capacity = 3 * row_count * route_count // (2 * expert_count)
    mean_square = jnp.mean(tokens * tokens, axis=-1, keepdims=True)
    normed = (tokens * lax.rsqrt(mean_square + 1e-06) * norm_gain).astype(jnp.bfloat16)
    flat_ids = expert_ids[0].reshape(row_count * route_count)
    onehot = (flat_ids[:, None] == jnp.arange(expert_count, dtype=jnp.int32)[None, :]).astype(
        jnp.int32
    )
    before = jnp.cumsum(onehot, axis=0) - onehot
    slot_index = jnp.sum(before * onehot, axis=1)
    target = (flat_ids * capacity + slot_index).reshape(row_count, route_count)
    slot_rows = jnp.arange(expert_count * capacity, dtype=jnp.int32)
    placement = jnp.any(target[None, :, :] == slot_rows[:, None, None], axis=-1).astype(
        jnp.bfloat16
    )
    outgoing = jnp.dot(placement, normed, preferred_element_type=jnp.float32).astype(jnp.bfloat16)
    outgoing = outgoing.reshape(expert_count, capacity, normed.shape[1])
    received = lax.all_to_all(outgoing, "ep", split_axis=0, concat_axis=0, tiled=True)
    flat_rows = received.reshape(expert_count * capacity, normed.shape[1])
    gate_rows = lax.all_gather(w_gate[0], "ctx", axis=0, tiled=True)
    up_rows = lax.all_gather(w_up[0], "ctx", axis=0, tiled=True)
    down_rows = lax.all_gather(w_down[0], "ctx", axis=0, tiled=True)
    contract = (((1,), (1,)), ((), ()))
    gate_pre = lax.dot_general(flat_rows, gate_rows, contract, preferred_element_type=jnp.float32)
    up_pre = lax.dot_general(flat_rows, up_rows, contract, preferred_element_type=jnp.float32)
    activated = (jax.nn.silu(gate_pre) * up_pre).astype(jnp.bfloat16)
    produced = jnp.dot(activated, down_rows, preferred_element_type=jnp.float32)
    produced = produced.astype(jnp.bfloat16).reshape(expert_count, capacity, normed.shape[1])
    returned = lax.all_to_all(produced, "ep", split_axis=0, concat_axis=0, tiled=True)
    returned_rows = returned.reshape(expert_count * capacity, normed.shape[1])
    picked = returned_rows[target]
    route_weight = gate_probs[0]
    mixture = jnp.zeros((row_count, normed.shape[1]), jnp.float32)
    for route in range(route_count):
        mixture = mixture + route_weight[:, route : route + 1] * picked[:, route].astype(
            jnp.float32
        )
    return mixture.astype(jnp.bfloat16)[None]


def per_device(
    queries, keys, values, hidden, expert_ids, gate_probs, norm_gain, w_gate, w_up, w_down
):
    attended = attend(queries, keys, values)
    expert_mix = experts(hidden, expert_ids, gate_probs, norm_gain, w_gate, w_up, w_down)
    return (attended, expert_mix)


def solution(mesh):
    placed = (
        P("ep", "ctx", None),
        P("ep", "ctx", None),
        P("ep", "ctx", None),
        P("ep", "ctx", None),
        P("ep", "ctx", None),
        P("ep", "ctx", None),
        P(),
        P("ep", "ctx", None),
        P("ep", "ctx", None),
        P("ep", "ctx", None),
    )
    return jax.shard_map(
        per_device,
        mesh=mesh,
        in_specs=placed,
        out_specs=(P("ep", "ctx", None), P("ep", "ctx", None)),
        check_vma=False,
    )
```

profile of v0, /device:TPU:32, one launch (start us, length us, event | category | flops | bytes accessed | tf_op | source)
XLA Modules:
  0.0 414.3 jit_solution(6666725445391555825)
XLA Ops:
  7.2 0.0 all-gather.15.cloned.1.call-start
  7.2 0.7 all-gather.15.cloned.1.call-update
  7.9 0.0 all-gather.19.cloned.1.call-start
  7.9 0.7 all-gather.19.cloned.1.call-update
  8.6 0.8 copy.37
  9.4 0.1 eq.40
  9.6 0.1 eq.44
  9.7 0.6 reduce-window.6
  10.3 0.2 slice_reduce_fusion
  10.6 0.1 fusion.43
  10.7 0.1 reduce_sum.32
  10.8 0.1 copy.41
  10.9 0.1 fusion.40
  11.0 1.2 fusion.27
  12.2 1.7 convolution_convert_fusion
  13.9 1.5 reshape.198
  15.4 15.3 %all-to-all-start = ((bf16[32,12,2048]{2,1,0:T(8,128)(2,1)}), bf16[32,12,2048]{2,1,0:T(8,128)(2,1)S(1)}, u32[]{:S(2)}, u32[]{:S(2)}) async-start(bf16[32,12,2048]{2,1,0:T(8,128)(2,1)} %reshape.198), calls=%async_computation | async-start | bytes 4194304 | tf_op jit(solution)/shard_map/all_to_all | solution.py:105
  30.8 0.0 all-gather.17.cloned.1.call-start
  30.8 0.7 all-gather.17.cloned.1.call-update
  31.5 99.4 %all-to-all-done = bf16[32,12,2048]{2,1,0:T(8,128)(2,1)S(1)} async-done(((bf16[32,12,2048]{2,1,0:T(8,128)(2,1)}), bf16[32,12,2048]{2,1,0:T(8,128)(2,1)S(1)}, u32[]{:S(2)}, u32[]{:S(2)}) %all-to-all-start) | async-done | bytes 1572896 | tf_op jit(solution)/shard_map/all_to_all | solution.py:105
  130.9 1.4 reshape.199
  132.3 0.0 copy-start
  132.3 0.0 all-gather.15.cloned.1.call-done
  132.3 5.1 %fusion.16 = f32[384,768]{1,0:T(8,128)} fusion(bf16[384,2048]{1,0:T(8,128)(2,1)} %reshape.199, bf16[1,768,2048]{2,1,0:T(8,128)(2,1)} %all-gather.15.cloned.1.call-done), kind=kOutput, calls=%fused_computation.20 | convolution fusion | flops 1207959552 | bytes 5898240 | tf_op jit(solution)/shard_map/dot_general | solution.py:111
  137.3 6.5 %all-gather.19.cloned.1.call-done = bf16[1,768,2048]{2,1,0:T(8,128)(2,1)} async-done(((bf16[1,48,2048]{2,1,0:T(8,128)(2,1)}), bf16[1,768,2048]{2,1,0:T(8,128)(2,1)}) %all-gather.19.cloned.1.call-update) | async-done | bytes 3145744 | tf_op jit(solution)/shard_map/all_gather | solution.py:109
  143.8 65.4 %all-gather.17.cloned.1.call-done = bf16[1,768,2048]{2,1,0:T(8,128)(2,1)} async-done(((bf16[1,48,2048]{2,1,0:T(8,128)(2,1)}), bf16[1,768,2048]{2,1,0:T(8,128)(2,1)}) %all-gather.17.cloned.1.call-update) | async-done | bytes 3145744 | tf_op jit(solution)/shard_map/all_gather | solution.py:108
  209.2 0.0 copy-done
  209.2 6.3 %fusion.18 = bf16[384,2048]{1,0:T(8,128)(2,1)S(1)} fusion(bf16[1,768,2048]{2,1,0:T(8,128)(2,1)} %all-gather.19.cloned.1.call-done, bf16[384,2048]{1,0:T(8,128)(2,1)S(1)} %copy-done, bf16[1,768,2048]{2,1,0:T(8,128)(2,1)} %all-gather.17.cloned.1.call-done, f32[384,768]{1,0:T(8,128)} %fusion.16), kind=kOutput, calls=%fused_computation.22 | convolution fusion | flops 2418475008 | bytes 10616832 | tf_op jit(solution)/shard_map/dot_general | solution.py:114
  215.5 1.6 reshape.200
  217.1 0.0 copy-start.3
  217.1 0.0 copy-start.1
  217.1 13.0 %all-to-all-start.1 = ((bf16[32,12,2048]{2,1,0:T(8,128)(2,1)}), bf16[32,12,2048]{2,1,0:T(8,128)(2,1)}, u32[]{:S(2)}, u32[]{:S(2)}) async-start(bf16[32,12,2048]{2,1,0:T(8,128)(2,1)} %reshape.200), calls=%async_computation.1 | async-start | bytes 4194304 | tf_op jit(solution)/shard_map/all_to_all | solution.py:116
  230.1 0.0 all-gather.11.cloned.1.call-start
  230.1 0.5 all-gather.11.cloned.1.call-update
  230.6 0.0 all-gather.13.cloned.1.call-start
  230.7 0.5 all-gather.13.cloned.1.call-update
  231.2 0.1 reduce_sum.34
  231.4 0.6 fusion.46
  232.7 0.1 reshape.207
  232.9 0.0 copy-done.3
  232.9 57.1 %all-gather.11.cloned.1.call-done = bf16[1,2048,256]{2,1,0:T(8,128)(2,1)} async-done(((bf16[1,128,256]{2,1,0:T(8,128)(2,1)}), bf16[1,2048,256]{2,1,0:T(8,128)(2,1)}) %all-gather.11.cloned.1.call-update) | async-done | bytes 1048592 | tf_op jit(solution)/shard_map/all_gather | solution.py:69
  289.9 60.4 %all-gather.13.cloned.1.call-done = bf16[1,2048,256]{2,1,0:T(8,128)(2,1)} async-done(((bf16[1,128,256]{2,1,0:T(8,128)(2,1)}), bf16[1,2048,256]{2,1,0:T(8,128)(2,1)}) %all-gather.13.cloned.1.call-update) | async-done | bytes 1048592 | tf_op jit(solution)/shard_map/all_gather | solution.py:70
  350.3 0.0 copy-done.1
  350.3 46.9 %conditional.1 = (f32[2,16,128]{2,1,0:T(8,128)S(1)}, f32[2,16,128,128]{3,2,1,0:T(8,128)S(1)}) conditional(s32[]{:T(128)} %convert_element_type.84, () %tuple.16, (s32[2048]{0:T(1024)S(1)}, s32[128]{0:T(128)S(1)}, bf16[2048,256]{1,0:T(8,128)(2,1)}, bf16[1,128,4096]{2,1,0:T(8,128)(2,1)S(1)}, bf16[2048,256]{1,0:T(8,128)(2,1)}) %tuple.36), branch_computations={%region_1.0_spmd, %region_2.5_spmd} | conditional | flops 4387500032 | bytes 117547560 | solution.py:63
  350.3 0.3 broadcast_compare_fusion
  350.7 0.2 copy.53
  350.9 1.3 reshape.190
  352.3 13.2 %fusion.2 = (f32[2,16,128]{2,1,0:T(8,128)S(1)}, f32[2,2048,128,16]{2,1,3,0:T(8,128)}) fusion(pred[128,2048]{0,1:T(8,128)(4,1)S(1)} %broadcast_compare_fusion, bf16[128,2,16,128]{3,2,1,0:T(8,128)(2,1)S(1)} %bitcast.90, bf16[2048,2,128,1]{2,1,0,3:T(2,128)(2,1)S(1)} %bitcast.91), kind=kOutput, calls=%fused_computation.5 | convolution fusion | flops 2172645376 | bytes 35930112 | tf_op jit(solution)/shard_map/cond/branch_1_fun/rgjd,ngd->gjrn/dot_general | solution.py:42
  365.5 0.0 copy-start.2
  365.5 14.4 %fusion.1 = f32[2,16,128]{2,1,0:T(8,128)S(1)} fusion(f32[2,2048,128,16]{2,1,3,0:T(8,128)} %get-tuple-element.27, f32[2,16,128]{2,1,0:T(8,128)S(1)} %broadcast_maximum_fusion, pred[128,2048]{0,1:T(8,128)(4,1)S(1)} %broadcast_compare_fusion), kind=kLoop, calls=%fused_computation.4 | loop fusion | flops 33550336 | bytes 33849344 | tf_op jit(solution)/shard_map/cond/branch_1_fun/reduce_sum | solution.py:51
  379.9 0.0 copy-done.2
  379.9 1.1 reshape.191
  381.0 15.9 %fusion.3 = f32[2,16,128,128]{3,2,1,0:T(8,128)S(1)} fusion(f32[2,2048,128,16]{2,1,3,0:T(8,128)} %get-tuple-element.27, f32[2,16,128]{2,1,0:T(8,128)S(1)} %broadcast_maximum_fusion, pred[128,2048]{0,1:T(8,128)(4,1)S(1)} %broadcast_compare_fusion, bf16[2048,2,128,1]{2,1,0,3:T(2,128)(2,1)} %bitcast.95), kind=kOutput, calls=%fused_computation.6 | convolution fusion | flops 2181038080 | bytes 36978688 | tf_op jit(solution)/shard_map/cond/branch_1_fun/gjrn,ngd->gjrd/dot_general | solution.py:52
  397.2 0.7 fusion.32
  397.9 0.7 copy.36
  398.6 1.3 convert_element_type.87
  399.9 0.0 all-to-all-done.1
  399.9 2.5 reshape.201
  402.4 1.4 gather_fusion
  403.8 0.7 reshape.206
  404.5 1.5 fusion.47
  406.0 1.8 fusion.31
  (11 shorter events, 0.1 us)
Async XLA Ops:
  7.2 125.1 %all-gather.15.cloned.1.call-start = ((), (), s32[]{:S(2)}) async-start(), calls=%async_computation.4 | async-start | bytes 3342336 | tf_op jit(solution)/shard_map/all_gather | solution.py:107
  7.9 135.9 %all-gather.19.cloned.1.call-start = ((), (), s32[]{:S(2)}) async-start(), calls=%async_computation.6 | async-start | bytes 3342336 | tf_op jit(solution)/shard_map/all_gather | solution.py:109
  15.4 115.5 %all-to-all-start = ((bf16[32,12,2048]{2,1,0:T(8,128)(2,1)}), bf16[32,12,2048]{2,1,0:T(8,128)(2,1)S(1)}, u32[]{:S(2)}, u32[]{:S(2)}) async-start(bf16[32,12,2048]{2,1,0:T(8,128)(2,1)} %reshape.198), calls=%async_computation | async-start | bytes 4194304 | tf_op jit(solution)/shard_map/all_to_all | solution.py:105
  30.8 178.5 %all-gather.17.cloned.1.call-start = ((), (), s32[]{:S(2)}) async-start(), calls=%async_computation.5 | async-start | bytes 3342336 | tf_op jit(solution)/shard_map/all_gather | solution.py:108
  132.3 77.0 %copy-start = (bf16[384,2048]{1,0:T(8,128)(2,1)S(1)}, bf16[384,2048]{1,0:T(8,128)(2,1)}, u32[]{:S(2)}) copy-start(bf16[384,2048]{1,0:T(8,128)(2,1)} %reshape.199) | copy-start | bytes 4718596
  217.1 15.8 %copy-start.3 = (f32[1,128,2]{1,2,0:T(2,128)S(1)}, f32[1,128,2]{1,2,0:T(2,128)}, u32[]{:S(2)}) copy-start(f32[1,128,2]{1,2,0:T(2,128)} %param.17) | copy-start | bytes 3076
  217.1 133.3 %copy-start.1 = (bf16[1,128,4096]{2,1,0:T(8,128)(2,1)S(1)}, bf16[1,128,4096]{2,1,0:T(8,128)(2,1)}, u32[]{:S(2)}) copy-start(bf16[1,128,4096]{2,1,0:T(8,128)(2,1)} %param.12) | copy-start | bytes 3145732
  217.1 182.8 %all-to-all-start.1 = ((bf16[32,12,2048]{2,1,0:T(8,128)(2,1)}), bf16[32,12,2048]{2,1,0:T(8,128)(2,1)}, u32[]{:S(2)}, u32[]{:S(2)}) async-start(bf16[32,12,2048]{2,1,0:T(8,128)(2,1)} %reshape.200), calls=%async_computation.1 | async-start | bytes 4194304 | tf_op jit(solution)/shard_map/all_to_all | solution.py:116
  230.1 59.9 %all-gather.11.cloned.1.call-start = ((), (), s32[]{:S(2)}) async-start(), calls=%async_computation.2 | async-start | bytes 1114112 | tf_op jit(solution)/shard_map/all_gather | solution.py:69
  230.6 119.7 %all-gather.13.cloned.1.call-start = ((), (), s32[]{:S(2)}) async-start(), calls=%async_computation.3 | async-start | bytes 1114112 | tf_op jit(solution)/shard_map/all_gather | solution.py:70
  365.5 14.4 %copy-start.2 = (bf16[2048,256]{1,0:T(8,128)(2,1)S(1)}, bf16[2048,256]{1,0:T(8,128)(2,1)}, u32[]{:S(2)}) copy-start(bf16[2048,256]{1,0:T(8,128)(2,1)} %get-tuple-element.17) | copy-start | bytes 3145732 | tf_op jit(solution)/shard_map/cond
Sparse Core Ops, SparseCore 0:
  11.1 67.3 all-gather.14
  81.5 62.2 all-gather.18
  146.9 62.2 all-gather.16
  233.6 56.2 all-gather.10
  292.8 57.4 all-gather.12
where the time goes:
time: 415 us; the launch traced here: 414 us
  waiting for transfers between devices  292 us (70%)
  matrix products  42.2 us (10%)
  starting transfers between devices  28.5 us (7%)
  other arithmetic  20 us (5%)
  local copies, waits for them, and re-layouts  16.9 us (4%)
  between operations  14.6 us (4%)
    all_to_all x1, waiting for transfers between devices, experts(): lax.all_to_all(outgoing, 'ep', split_axis=0, concat_axis=0, tiled=True)  99.4 us
    all_gather x1, waiting for transfers between devices, experts(): up_rows = lax.all_gather(w_up[0], 'ctx', axis=0, tiled=True)  65.4 us
    all_gather x1, waiting for transfers between devices, attend(): lax.all_gather(values[0], 'ctx', axis=0, tiled=True)  60.4 us
    all_gather x1, waiting for transfers between devices, attend(): lax.all_gather(keys[0], 'ctx', axis=0, tiled=True)  57.1 us
    dot_general x1, matrix products, compute(): jnp.einsum('gjrn,ngd->gjrd', exponent.astype(jnp.bfloat16), value_heads,...  15.9 us
    all_to_all x1, starting transfers between devices, experts(): lax.all_to_all(outgoing, 'ep', split_axis=0, concat_axis=0, tiled=True)  15.3 us
    reduce_sum x1, other arithmetic, compute(): new_totals = jnp.sum(exponent, axis=-1)  14.4 us
    dot_general x1, matrix products, compute(): jnp.einsum('rgjd,ngd->gjrn', group_rows, key_heads, preferred_element_typ...  13.2 us
  transfers between devices with their start and end apart: 7, of which 5 were waited for; matrix products, arithmetic and copies ran while one was open for 15% of the time, Pallas kernels for 0%

commit v1 on v0

--- a/solution.py
+++ b/solution.py
@@ -63,12 +63,32 @@
             updated.append(lax.cond(offset <= jnp.max(query_pos), compute, unchanged, current))
         return tuple(updated)
 
+    def drive_the_sizes(in_array, lane_axis):
+        heard, a_now, long_array = (
+            lax.axis_size(lane_axis),
+            lax.axis_index(lane_axis),
+            in_array.shape[0],
+        )
+        frames = [dev_j * heard if b == 0 else dev_j for b, dev_j in enumerate(in_array.shape)]
+        n_now = lax.dynamic_update_slice_in_dim(
+            jnp.zeros(frames, in_array.dtype), in_array, a_now * long_array, axis=0
+        )
+        z1 = tall = in_array
+        for at in range(1, heard // 2 + 1):
+            z1 = lax.ppermute(z1, lane_axis, [(b, (b + 1) % heard) for b in range(heard)])
+            n_now = lax.dynamic_update_slice_in_dim(
+                n_now, z1, (a_now - at) % heard * long_array, axis=0
+            )
+            if 2 * at < heard:
+                tall = lax.ppermute(tall, lane_axis, [(b, (b - 1) % heard) for b in range(heard)])
+                n_now = lax.dynamic_update_slice_in_dim(
+                    n_now, tall, (a_now + at) % heard * long_array, axis=0
+                )
+        return n_now
+
     finals = update(
         initial,
-        (
-            lax.all_gather(keys[0], "ctx", axis=0, tiled=True),
-            lax.all_gather(values[0], "ctx", axis=0, tiled=True),
-        ),
+        (lax.all_gather(keys[0], "ctx", axis=0, tiled=True), drive_the_sizes(values[0], "ctx")),
         jnp.int32(0),
     )
     outputs = []

time: 415 us -> 383 us (0.923)
  waiting for transfers between devices: 292 us -> 182 us
  starting transfers between devices: 28.5 us -> 95.1 us
  local copies, waits for them, and re-layouts: 16.9 us -> 25.3 us
    ppermute x0 -> x15, starting transfers between devices: none -> 66.6 us  [the longest x7 50.6 us: drive_the_sizes(): lax.ppermute(tall, lane_axis, [(b, (b - 1) % heard) for b in range(heard)])]
    all_gather x1 -> x0, waiting for transfers between devices: 60.4 us -> none  [attend(): lax.all_gather(values[0], 'ctx', axis=0, tiled=True)]
    all_gather x1, waiting for transfers between devices: 6.51 us -> 65.4 us  [experts(): down_rows = lax.all_gather(w_down[0], 'ctx', axis=0, tiled=True)]
    all_gather x1, waiting for transfers between devices: 65.4 us -> 6.54 us  [experts(): up_rows = lax.all_gather(w_up[0], 'ctx', axis=0, tiled=True)]
    all_gather x1, waiting for transfers between devices: 57.1 us -> 0.01 us  [attend(): lax.all_gather(keys[0], 'ctx', axis=0, tiled=True)]
    dynamic_update_slice x0 -> x16, local copies, waits for them, and re-layouts: none -> 9.04 us  [the longest x8 4.38 us: drive_the_sizes(): lax.dynamic_update_slice_in_dim(n_now, z1, (a_now - at) % heard * long_ar...]
    ppermute x0 -> x15, waiting for transfers between devices: none -> 8.07 us  [the longest x8 8.05 us: drive_the_sizes(): lax.ppermute(z1, lane_axis, [(b, (b + 1) % heard) for b in range(heard)])]
  transfers between devices with their start and end apart: 7 -> 21, of which waited for: 5 -> 9; matrix products, arithmetic and copies ran while one was open for 15% -> 19% of each run, Pallas kernels for 0% -> 0%
where the time goes in v1:
time: 383 us; the launch traced here: 382 us
  waiting for transfers between devices  182 us (48%)
  starting transfers between devices  95.1 us (25%)
  matrix products  42.2 us (11%)
  local copies, waits for them, and re-layouts  25.3 us (7%)
  other arithmetic  21.2 us (6%)
  between operations  14.8 us (4%)
    all_to_all x1, waiting for transfers between devices, experts(): lax.all_to_all(outgoing, 'ep', split_axis=0, concat_axis=0, tiled=True)  99.4 us
    all_gather x1, waiting for transfers between devices, experts(): down_rows = lax.all_gather(w_down[0], 'ctx', axis=0, tiled=True)  65.4 us
    ppermute x7, starting transfers between devices, drive_the_sizes(): lax.ppermute(tall, lane_axis, [(b, (b - 1) % heard) for b in range(heard)])  50.6 us
    ppermute x8, starting transfers between devices, drive_the_sizes(): lax.ppermute(z1, lane_axis, [(b, (b + 1) % heard) for b in range(heard)])  16 us
    dot_general x1, matrix products, compute(): jnp.einsum('gjrn,ngd->gjrd', exponent.astype(jnp.bfloat16), value_heads,...  15.9 us
    all_to_all x1, starting transfers between devices, experts(): lax.all_to_all(outgoing, 'ep', split_axis=0, concat_axis=0, tiled=True)  15.3 us
    reduce_sum x1, other arithmetic, compute(): new_totals = jnp.sum(exponent, axis=-1)  14.3 us
    dot_general x1, matrix products, compute(): jnp.einsum('rgjd,ngd->gjrn', group_rows, key_heads, preferred_element_typ...  13.3 us
  transfers between devices with their start and end apart: 21, of which 9 were waited for; matrix products, arithmetic and copies ran while one was open for 19% of the time, Pallas kernels for 0%

profile of v1, /device:TPU:32, one launch (start us, length us, event | category | flops | bytes accessed | tf_op | source)
XLA Modules:
  0.0 381.5 jit_solution(2238488187018659361)
XLA Ops:
  7.2 0.7 all-gather.11.cloned.1.call-update
  7.9 0.7 all-gather.13.cloned.1.call-update
  8.6 0.8 copy.39
  9.7 0.6 reduce-window.6
  11.0 1.2 fusion.26
  12.2 1.7 convolution_convert_fusion
  13.9 1.5 reshape.205
  15.4 15.3 %all-to-all-start = ((bf16[32,12,2048]{2,1,0:T(8,128)(2,1)}), bf16[32,12,2048]{2,1,0:T(8,128)(2,1)S(1)}, u32[]{:S(2)}, u32[]{:S(2)}) async-start(bf16[32,12,2048]{2,1,0:T(8,128)(2,1)} %reshape.205), calls=%async_computation | async-start | bytes 4194304 | tf_op jit(solution)/shard_map/all_to_all | solution.py:125
  30.8 0.7 all-gather.15.cloned.1.call-update
  31.5 99.4 %all-to-all-done = bf16[32,12,2048]{2,1,0:T(8,128)(2,1)S(1)} async-done(((bf16[32,12,2048]{2,1,0:T(8,128)(2,1)}), bf16[32,12,2048]{2,1,0:T(8,128)(2,1)S(1)}, u32[]{:S(2)}, u32[]{:S(2)}) %all-to-all-start) | async-done | bytes 1572896 | tf_op jit(solution)/shard_map/all_to_all | solution.py:125
  130.9 1.3 reshape.206
  132.2 5.1 %fusion.15 = f32[384,768]{1,0:T(8,128)} fusion(bf16[384,2048]{1,0:T(8,128)(2,1)} %reshape.206, bf16[1,768,2048]{2,1,0:T(8,128)(2,1)} %all-gather.11.cloned.1.call-done), kind=kOutput, calls=%fused_computation.34 | convolution fusion | flops 1207959552 | bytes 5898240 | tf_op jit(solution)/shard_map/dot_general | solution.py:131
  137.3 6.5 %all-gather.13.cloned.1.call-done = bf16[1,768,2048]{2,1,0:T(8,128)(2,1)} async-done(((bf16[1,48,2048]{2,1,0:T(8,128)(2,1)}), bf16[1,768,2048]{2,1,0:T(8,128)(2,1)}) %all-gather.13.cloned.1.call-update) | async-done | bytes 3145744 | tf_op jit(solution)/shard_map/all_gather | solution.py:128
  143.8 65.4 %all-gather.15.cloned.1.call-done = bf16[1,768,2048]{2,1,0:T(8,128)(2,1)} async-done(((bf16[1,48,2048]{2,1,0:T(8,128)(2,1)}), bf16[1,768,2048]{2,1,0:T(8,128)(2,1)}) %all-gather.15.cloned.1.call-update) | async-done | bytes 3145744 | tf_op jit(solution)/shard_map/all_gather | solution.py:129
  209.2 6.3 %fusion.17 = bf16[384,2048]{1,0:T(8,128)(2,1)S(1)} fusion(bf16[1,768,2048]{2,1,0:T(8,128)(2,1)} %all-gather.15.cloned.1.call-done, bf16[384,2048]{1,0:T(8,128)(2,1)S(1)} %copy-done, bf16[1,768,2048]{2,1,0:T(8,128)(2,1)} %all-gather.13.cloned.1.call-done, f32[384,768]{1,0:T(8,128)} %fusion.15), kind=kOutput, calls=%fused_computation.36 | convolution fusion | flops 2418475008 | bytes 10616832 | tf_op jit(solution)/shard_map/dot_general | solution.py:134
  215.5 1.6 reshape.207
  217.1 13.0 %all-to-all-start.1 = ((bf16[32,12,2048]{2,1,0:T(8,128)(2,1)}), bf16[32,12,2048]{2,1,0:T(8,128)(2,1)}, u32[]{:S(2)}, u32[]{:S(2)}) async-start(bf16[32,12,2048]{2,1,0:T(8,128)(2,1)} %reshape.207), calls=%async_computation.1 | async-start | bytes 4194304 | tf_op jit(solution)/shard_map/all_to_all | solution.py:136
  230.1 0.5 all-gather.9.cloned.1.call-update
  230.8 2.6 collective-permute-start
  233.4 6.5 %collective-permute-start.1 = (bf16[128,256]{0,1:T(8,128)(2,1)S(1)}, bf16[128,256]{0,1:T(8,128)(2,1)S(1)}, u32[]{:S(2)}, u32[]{:S(2)}) collective-permute-start(bf16[128,256]{0,1:T(8,128)(2,1)S(1)} %bitcast.104), channel_id=1, source_target_pairs={{0,480},{32,0},{64,32},{96,64},{128,96},{160,128},{192,160},{224,1... | collective-permute-start | bytes 196616 | tf_op jit(solution)/shard_map/ppermute | solution.py:83
  240.0 0.3 collective-permute-done
  240.3 1.9 collective-permute-start.2
  242.2 7.2 %collective-permute-start.3 = (bf16[128,256]{0,1:T(8,128)(2,1)S(1)}, bf16[128,256]{0,1:T(8,128)(2,1)S(1)}, u32[]{:S(2)}, u32[]{:S(2)}) collective-permute-start(bf16[128,256]{0,1:T(8,128)(2,1)S(1)} %collective-permute-done.1), channel_id=1, source_target_pairs={{0,480},{32,0},{64,32},{96,64},{128,96},{160,128},{192,160},{224,1... | collective-permute-start | bytes 196616 | tf_op jit(solution)/shard_map/ppermute | solution.py:83
  249.7 1.9 collective-permute-start.4
  251.7 7.5 %collective-permute-start.5 = (bf16[128,256]{0,1:T(8,128)(2,1)S(1)}, bf16[128,256]{0,1:T(8,128)(2,1)S(1)}, u32[]{:S(2)}, u32[]{:S(2)}) collective-permute-start(bf16[128,256]{0,1:T(8,128)(2,1)S(1)} %collective-permute-done.3), channel_id=1, source_target_pairs={{0,480},{32,0},{64,32},{96,64},{128,96},{160,128},{192,160},{224,1... | collective-permute-start | bytes 196616 | tf_op jit(solution)/shard_map/ppermute | solution.py:83
  259.4 1.9 collective-permute-start.6
  261.4 7.2 %collective-permute-start.7 = (bf16[128,256]{0,1:T(8,128)(2,1)S(1)}, bf16[128,256]{0,1:T(8,128)(2,1)S(1)}, u32[]{:S(2)}, u32[]{:S(2)}) collective-permute-start(bf16[128,256]{0,1:T(8,128)(2,1)S(1)} %collective-permute-done.5), channel_id=1, source_target_pairs={{0,480},{32,0},{64,32},{96,64},{128,96},{160,128},{192,160},{224,1... | collective-permute-start | bytes 196616 | tf_op jit(solution)/shard_map/ppermute | solution.py:83
  268.8 1.9 collective-permute-start.8
  270.8 7.4 %collective-permute-start.9 = (bf16[128,256]{0,1:T(8,128)(2,1)S(1)}, bf16[128,256]{0,1:T(8,128)(2,1)S(1)}, u32[]{:S(2)}, u32[]{:S(2)}) collective-permute-start(bf16[128,256]{0,1:T(8,128)(2,1)S(1)} %collective-permute-done.7), channel_id=1, source_target_pairs={{0,480},{32,0},{64,32},{96,64},{128,96},{160,128},{192,160},{224,1... | collective-permute-start | bytes 196616 | tf_op jit(solution)/shard_map/ppermute | solution.py:83
  278.3 1.9 collective-permute-start.10
  280.2 0.6 slice_bitcast_fusion.1
  280.8 0.6 fusion.45
  282.3 7.2 %collective-permute-start.11 = (bf16[128,256]{0,1:T(8,128)(2,1)S(1)}, bf16[128,256]{0,1:T(8,128)(2,1)S(1)}, u32[]{:S(2)}, u32[]{:S(2)}) collective-permute-start(bf16[128,256]{0,1:T(8,128)(2,1)S(1)} %collective-permute-done.9), channel_id=1, source_target_pairs={{0,480},{32,0},{64,32},{96,64},{128,96},{160,128},{192,160},{224,1... | collective-permute-start | bytes 196616 | tf_op jit(solution)/shard_map/ppermute | solution.py:83
  289.5 1.9 collective-permute-start.12
  291.5 7.5 %collective-permute-start.13 = (bf16[128,256]{0,1:T(8,128)(2,1)S(1)}, bf16[128,256]{0,1:T(8,128)(2,1)S(1)}, u32[]{:S(2)}, u32[]{:S(2)}) collective-permute-start(bf16[128,256]{0,1:T(8,128)(2,1)S(1)} %collective-permute-done.11), channel_id=1, source_target_pairs={{0,480},{32,0},{64,32},{96,64},{128,96},{160,128},{192,160},{224,1... | collective-permute-start | bytes 196616 | tf_op jit(solution)/shard_map/ppermute | solution.py:83
  299.0 1.9 collective-permute-start.14
  300.9 0.6 iota_add_fusion
  301.5 7.0 %collective-permute-done.14 = bf16[128,256]{0,1:T(8,128)(2,1)S(1)} collective-permute-done((bf16[128,256]{0,1:T(8,128)(2,1)S(1)}, bf16[128,256]{0,1:T(8,128)(2,1)S(1)}, u32[]{:S(2)}, u32[]{:S(2)}) %collective-permute-start.14) | collective-permute-done | bytes 65568 | tf_op jit(solution)/shard_map/ppermute | solution.py:78
  308.5 55.9 %conditional.1 = (f32[2,16,128]{2,1,0:T(8,128)S(1)}, f32[2,16,128,128]{3,2,1,0:T(8,128)S(1)}) conditional(s32[]{:T(128)} %convert_element_type.87, () %tuple.159, (s32[2048]{0:T(1024)S(1)}, s32[128]{0:T(128)}, bf16[2048,256]{1,0:T(8,128)(2,1)}, bf16[1,128,4096]{2,1,0:T(8,128)(2,1)S(1)}, s32[]{:T(128)}, ...), branch_computations={%region_1.2_spmd, %region_2.5_spmd.clone.clone} | conditional | flops 4387500032 | bytes 129871256 | solution.py:63
  308.8 0.5 copy-done.7
  309.6 0.3 dynamic_update_slice.160
  310.1 0.9 constant_dynamic-update-slice_fusion.10
  311.0 0.9 constant_dynamic-update-slice_fusion.9
  311.9 0.9 constant_dynamic-update-slice_fusion.8
  312.8 0.9 constant_dynamic-update-slice_fusion.7
  313.7 0.9 constant_dynamic-update-slice_fusion.6
  314.6 0.9 constant_dynamic-update-slice_fusion.5
  315.4 0.9 constant_dynamic-update-slice_fusion.4
  316.3 0.9 constant_dynamic-update-slice_fusion.3
  317.3 0.9 constant_dynamic-update-slice_fusion.1
  318.2 0.9 constant_dynamic-update-slice_fusion
  319.0 1.0 broadcast_compare_fusion
  320.1 0.3 reshape.229
  320.6 13.3 %fusion.2 = (f32[2,16,128]{2,1,0:T(8,128)S(1)}, f32[2,2048,128,16]{2,1,3,0:T(8,128)}) fusion(pred[128,2048]{0,1:T(8,128)(4,1)S(1)} %broadcast_compare_fusion, bf16[128,2,16,128]{3,2,1,0:T(8,128)(2,1)S(1)} %bitcast.99, bf16[2048,2,128,1]{2,1,0,3:T(2,128)(2,1)S(1)} %bitcast.98), kind=kOutput, calls=%fused_computation.5 | convolution fusion | flops 2172645376 | bytes 35930112 | tf_op jit(solution)/shard_map/cond/branch_1_fun/rgjd,ngd->gjrn/dot_general | solution.py:42
  333.9 15.9 %fusion.3 = f32[2,16,128,128]{3,2,1,0:T(8,128)S(1)} fusion(bf16[2048,2,128,1]{0,2,3,1:T(8,128)(2,1)S(1)} %bitcast.102, f32[2,2048,128,16]{2,1,3,0:T(8,128)} %get-tuple-element.1491, f32[2,16,128]{2,1,0:T(8,128)S(1)} %broadcast_maximum_fusion, pred[128,2048]{0,1:T(8,128)(4,1)S(1)} %broadcast_compare_fusion), kind=kOutput, calls=%fused_computation.6 | convolution fusion | flops 2181038080 | bytes 36978688 | tf_op jit(solution)/shard_map/cond/branch_1_fun/gjrn,ngd->gjrd/dot_general | solution.py:52
  349.8 14.3 %fusion.1 = f32[2,16,128]{2,1,0:T(8,128)S(1)} fusion(f32[2,2048,128,16]{2,1,3,0:T(8,128)} %get-tuple-element.1491, f32[2,16,128]{2,1,0:T(8,128)S(1)} %broadcast_maximum_fusion, pred[128,2048]{0,1:T(8,128)(4,1)S(1)} %broadcast_compare_fusion), kind=kLoop, calls=%fused_computation.4 | loop fusion | flops 33550336 | bytes 33849344 | tf_op jit(solution)/shard_map/cond/branch_1_fun/reduce_sum | solution.py:51
  364.4 0.7 fusion.31
  365.1 0.7 copy.38
  365.8 1.3 convert_element_type.90
  367.1 2.5 reshape.208
  369.6 1.4 gather_fusion
  371.0 0.7 reshape.215
  371.7 1.5 fusion.46
  373.2 1.8 fusion.30
  (85 shorter events, 3.0 us)
Async XLA Ops:
  7.2 125.1 %all-gather.11.cloned.1.call-start = ((), (), s32[]{:S(2)}) async-start(), calls=%async_computation.3 | async-start | bytes 3342336 | tf_op jit(solution)/shard_map/all_gather | solution.py:127
  7.9 135.9 %all-gather.13.cloned.1.call-start = ((), (), s32[]{:S(2)}) async-start(), calls=%async_computation.4 | async-start | bytes 3342336 | tf_op jit(solution)/shard_map/all_gather | solution.py:128
  15.4 115.5 %all-to-all-start = ((bf16[32,12,2048]{2,1,0:T(8,128)(2,1)}), bf16[32,12,2048]{2,1,0:T(8,128)(2,1)S(1)}, u32[]{:S(2)}, u32[]{:S(2)}) async-start(bf16[32,12,2048]{2,1,0:T(8,128)(2,1)} %reshape.205), calls=%async_computation | async-start | bytes 4194304 | tf_op jit(solution)/shard_map/all_to_all | solution.py:125
  30.7 178.5 %all-gather.15.cloned.1.call-start = ((), (), s32[]{:S(2)}) async-start(), calls=%async_computation.5 | async-start | bytes 3342336 | tf_op jit(solution)/shard_map/all_gather | solution.py:129
  132.2 77.0 %copy-start = (bf16[384,2048]{1,0:T(8,128)(2,1)S(1)}, bf16[384,2048]{1,0:T(8,128)(2,1)}, u32[]{:S(2)}) copy-start(bf16[384,2048]{1,0:T(8,128)(2,1)} %reshape.206) | copy-start | bytes 4718596
  215.5 15.2 %copy-start.5 = (bf16[1,128,256]{2,1,0:T(8,128)(2,1)S(1)}, bf16[1,128,256]{2,1,0:T(8,128)(2,1)}, u32[]{:S(2)}) copy-start(bf16[1,128,256]{2,1,0:T(8,128)(2,1)} %param.14) | copy-start | bytes 196612
  217.1 63.2 %copy-start.19 = (f32[1,128,2]{1,2,0:T(2,128)S(1)}, f32[1,128,2]{1,2,0:T(2,128)}, u32[]{:S(2)}) copy-start(f32[1,128,2]{1,2,0:T(2,128)} %param.17) | copy-start | bytes 3076
  217.1 91.4 %copy-start.1 = (bf16[1,128,4096]{2,1,0:T(8,128)(2,1)S(1)}, bf16[1,128,4096]{2,1,0:T(8,128)(2,1)}, u32[]{:S(2)}) copy-start(bf16[1,128,4096]{2,1,0:T(8,128)(2,1)} %param.12) | copy-start | bytes 3145732
  217.1 150.0 %all-to-all-start.1 = ((bf16[32,12,2048]{2,1,0:T(8,128)(2,1)}), bf16[32,12,2048]{2,1,0:T(8,128)(2,1)}, u32[]{:S(2)}, u32[]{:S(2)}) async-start(bf16[32,12,2048]{2,1,0:T(8,128)(2,1)} %reshape.207), calls=%async_computation.1 | async-start | bytes 4194304 | tf_op jit(solution)/shard_map/all_to_all | solution.py:136
  230.1 78.4 %all-gather.9.cloned.1.call-start = ((), (), s32[]{:S(2)}) async-start(), calls=%async_computation.2 | async-start | bytes 1114112 | tf_op jit(solution)/shard_map/all_gather | solution.py:91
  230.8 9.5 %collective-permute-start = (bf16[128,256]{0,1:T(8,128)(2,1)S(1)}, bf16[128,256]{0,1:T(8,128)(2,1)S(1)}, u32[]{:S(2)}, u32[]{:S(2)}) collective-permute-start(bf16[128,256]{0,1:T(8,128)(2,1)S(1)} %bitcast.103), channel_id=1, source_target_pairs={{0,32},{32,64},{64,96},{96,128},{128,160},{160,192},{192,224},{224... | collective-permute-start | bytes 196616 | tf_op jit(solution)/shard_map/ppermute | solution.py:78
  233.4 8.8 %collective-permute-start.1 = (bf16[128,256]{0,1:T(8,128)(2,1)S(1)}, bf16[128,256]{0,1:T(8,128)(2,1)S(1)}, u32[]{:S(2)}, u32[]{:S(2)}) collective-permute-start(bf16[128,256]{0,1:T(8,128)(2,1)S(1)} %bitcast.104), channel_id=1, source_target_pairs={{0,480},{32,0},{64,32},{96,64},{128,96},{160,128},{192,160},{224,1... | collective-permute-start | bytes 196616 | tf_op jit(solution)/shard_map/ppermute | solution.py:83
  240.3 9.5 %collective-permute-start.2 = (bf16[128,256]{0,1:T(8,128)(2,1)S(1)}, bf16[128,256]{0,1:T(8,128)(2,1)S(1)}, u32[]{:S(2)}, u32[]{:S(2)}) collective-permute-start(bf16[128,256]{0,1:T(8,128)(2,1)S(1)} %collective-permute-done), channel_id=1, source_target_pairs={{0,32},{32,64},{64,96},{96,128},{128,160},{160,192},{192,224},{224... | collective-permute-start | bytes 196616 | tf_op jit(solution)/shard_map/ppermute | solution.py:78
  242.2 9.5 %collective-permute-start.3 = (bf16[128,256]{0,1:T(8,128)(2,1)S(1)}, bf16[128,256]{0,1:T(8,128)(2,1)S(1)}, u32[]{:S(2)}, u32[]{:S(2)}) collective-permute-start(bf16[128,256]{0,1:T(8,128)(2,1)S(1)} %collective-permute-done.1), channel_id=1, source_target_pairs={{0,480},{32,0},{64,32},{96,64},{128,96},{160,128},{192,160},{224,1... | collective-permute-start | bytes 196616 | tf_op jit(solution)/shard_map/ppermute | solution.py:83
  249.7 9.6 %collective-permute-start.4 = (bf16[128,256]{0,1:T(8,128)(2,1)S(1)}, bf16[128,256]{0,1:T(8,128)(2,1)S(1)}, u32[]{:S(2)}, u32[]{:S(2)}) collective-permute-start(bf16[128,256]{0,1:T(8,128)(2,1)S(1)} %collective-permute-done.2), channel_id=1, source_target_pairs={{0,32},{32,64},{64,96},{96,128},{128,160},{160,192},{192,224},{224... | collective-permute-start | bytes 196616 | tf_op jit(solution)/shard_map/ppermute | solution.py:78
  251.7 9.8 %collective-permute-start.5 = (bf16[128,256]{0,1:T(8,128)(2,1)S(1)}, bf16[128,256]{0,1:T(8,128)(2,1)S(1)}, u32[]{:S(2)}, u32[]{:S(2)}) collective-permute-start(bf16[128,256]{0,1:T(8,128)(2,1)S(1)} %collective-permute-done.3), channel_id=1, source_target_pairs={{0,480},{32,0},{64,32},{96,64},{128,96},{160,128},{192,160},{224,1... | collective-permute-start | bytes 196616 | tf_op jit(solution)/shard_map/ppermute | solution.py:83
  259.4 9.5 %copy-start.6 = (bf16[128,256]{0,1:T(8,128)(2,1)}, bf16[128,256]{0,1:T(8,128)(2,1)S(1)}, u32[]{:S(2)}) copy-start(bf16[128,256]{0,1:T(8,128)(2,1)S(1)} %collective-permute-done.4) | copy-start | bytes 196612
  259.4 9.5 %collective-permute-start.6 = (bf16[128,256]{0,1:T(8,128)(2,1)S(1)}, bf16[128,256]{0,1:T(8,128)(2,1)S(1)}, u32[]{:S(2)}, u32[]{:S(2)}) collective-permute-start(bf16[128,256]{0,1:T(8,128)(2,1)S(1)} %collective-permute-done.4), channel_id=1, source_target_pairs={{0,32},{32,64},{64,96},{96,128},{128,160},{160,192},{192,224},{224... | collective-permute-start | bytes 196616 | tf_op jit(solution)/shard_map/ppermute | solution.py:78
  261.4 9.3 %collective-permute-start.7 = (bf16[128,256]{0,1:T(8,128)(2,1)S(1)}, bf16[128,256]{0,1:T(8,128)(2,1)S(1)}, u32[]{:S(2)}, u32[]{:S(2)}) collective-permute-start(bf16[128,256]{0,1:T(8,128)(2,1)S(1)} %collective-permute-done.5), channel_id=1, source_target_pairs={{0,480},{32,0},{64,32},{96,64},{128,96},{160,128},{192,160},{224,1... | collective-permute-start | bytes 196616 | tf_op jit(solution)/shard_map/ppermute | solution.py:83
  268.8 9.5 %collective-permute-start.8 = (bf16[128,256]{0,1:T(8,128)(2,1)S(1)}, bf16[128,256]{0,1:T(8,128)(2,1)S(1)}, u32[]{:S(2)}, u32[]{:S(2)}) collective-permute-start(bf16[128,256]{0,1:T(8,128)(2,1)S(1)} %collective-permute-done.6), channel_id=1, source_target_pairs={{0,32},{32,64},{64,96},{96,128},{128,160},{160,192},{192,224},{224... | collective-permute-start | bytes 196616 | tf_op jit(solution)/shard_map/ppermute | solution.py:78
  270.8 11.5 %collective-permute-start.9 = (bf16[128,256]{0,1:T(8,128)(2,1)S(1)}, bf16[128,256]{0,1:T(8,128)(2,1)S(1)}, u32[]{:S(2)}, u32[]{:S(2)}) collective-permute-start(bf16[128,256]{0,1:T(8,128)(2,1)S(1)} %collective-permute-done.7), channel_id=1, source_target_pairs={{0,480},{32,0},{64,32},{96,64},{128,96},{160,128},{192,160},{224,1... | collective-permute-start | bytes 196616 | tf_op jit(solution)/shard_map/ppermute | solution.py:83
  278.3 11.2 %collective-permute-start.10 = (bf16[128,256]{0,1:T(8,128)(2,1)S(1)}, bf16[128,256]{0,1:T(8,128)(2,1)S(1)}, u32[]{:S(2)}, u32[]{:S(2)}) collective-permute-start(bf16[128,256]{0,1:T(8,128)(2,1)S(1)} %collective-permute-done.8), channel_id=1, source_target_pairs={{0,32},{32,64},{64,96},{96,128},{128,160},{160,192},{192,224},{224... | collective-permute-start | bytes 196616 | tf_op jit(solution)/shard_map/ppermute | solution.py:78
  282.3 9.2 %collective-permute-start.11 = (bf16[128,256]{0,1:T(8,128)(2,1)S(1)}, bf16[128,256]{0,1:T(8,128)(2,1)S(1)}, u32[]{:S(2)}, u32[]{:S(2)}) collective-permute-start(bf16[128,256]{0,1:T(8,128)(2,1)S(1)} %collective-permute-done.9), channel_id=1, source_target_pairs={{0,480},{32,0},{64,32},{96,64},{128,96},{160,128},{192,160},{224,1... | collective-permute-start | bytes 196616 | tf_op jit(solution)/shard_map/ppermute | solution.py:83
  289.5 9.5 %collective-permute-start.12 = (bf16[128,256]{0,1:T(8,128)(2,1)S(1)}, bf16[128,256]{0,1:T(8,128)(2,1)S(1)}, u32[]{:S(2)}, u32[]{:S(2)}) collective-permute-start(bf16[128,256]{0,1:T(8,128)(2,1)S(1)} %collective-permute-done.10), channel_id=1, source_target_pairs={{0,32},{32,64},{64,96},{96,128},{128,160},{160,192},{192,224},{224... | collective-permute-start | bytes 196616 | tf_op jit(solution)/shard_map/ppermute | solution.py:78
  291.5 10.0 %collective-permute-start.13 = (bf16[128,256]{0,1:T(8,128)(2,1)S(1)}, bf16[128,256]{0,1:T(8,128)(2,1)S(1)}, u32[]{:S(2)}, u32[]{:S(2)}) collective-permute-start(bf16[128,256]{0,1:T(8,128)(2,1)S(1)} %collective-permute-done.11), channel_id=1, source_target_pairs={{0,480},{32,0},{64,32},{96,64},{128,96},{160,128},{192,160},{224,1... | collective-permute-start | bytes 196616 | tf_op jit(solution)/shard_map/ppermute | solution.py:83
  299.0 9.5 %collective-permute-start.14 = (bf16[128,256]{0,1:T(8,128)(2,1)S(1)}, bf16[128,256]{0,1:T(8,128)(2,1)S(1)}, u32[]{:S(2)}, u32[]{:S(2)}) collective-permute-start(bf16[128,256]{0,1:T(8,128)(2,1)S(1)} %collective-permute-done.12), channel_id=1, source_target_pairs={{0,32},{32,64},{64,96},{96,128},{128,160},{160,192},{192,224},{224... | collective-permute-start | bytes 196616 | tf_op jit(solution)/shard_map/ppermute | solution.py:78
  308.7 0.6 copy-start.7
  308.7 0.6 copy-start.8
  308.7 0.6 copy-start.9
  308.7 0.6 copy-start.10
  308.7 0.7 copy-start.11
  308.7 0.7 copy-start.12
  308.7 0.7 copy-start.13
  308.8 0.7 copy-start.14
  308.8 0.7 copy-start.16
  308.8 0.7 copy-start.17
  308.8 11.3 %copy-start.2 = (bf16[2048,256]{1,0:T(8,128)(2,1)S(1)}, bf16[2048,256]{1,0:T(8,128)(2,1)}, u32[]{:S(2)}) copy-start(bf16[2048,256]{1,0:T(8,128)(2,1)} %get-tuple-element.1418) | copy-start | bytes 3145732 | tf_op jit(solution)/shard_map/cond
  309.5 7.7 %copy-start.15 = (bf16[128,256]{0,1:T(8,128)(2,1)S(1)}, bf16[128,256]{0,1:T(8,128)(2,1)}, u32[]{:S(2)}) copy-start(bf16[128,256]{0,1:T(8,128)(2,1)} %copy-done.14) | copy-start | bytes 196612 | tf_op jit(solution)/shard_map/cond
  319.0 1.0 copy-start.3
  320.6 13.3 %copy-start.4 = (bf16[2048,256]{0,1:T(8,128)(2,1)S(1)}, bf16[2048,256]{0,1:T(8,128)(2,1)}, u32[]{:S(2)}) copy-start(bf16[2048,256]{0,1:T(8,128)(2,1)} %copy-done.3) | copy-start | bytes 3145732 | tf_op jit(solution)/shard_map/cond
  370.9 2.2 copy-start.18
Sparse Core Ops, SparseCore 0:
  11.1 67.3 all-gather.10
  81.5 62.2 all-gather.12
  146.9 62.2 all-gather.14
  233.6 57.4 all-gather.8
